TPU v7x, 1024 devices: a whole 8x8x8 slice. The times are simulated.
1024 devices in a mesh: dp: 16 (over z, core), ctx: 64 (over y, x).
Axes of the slice: x: 8, y: 8, z: 8, core: 2. Of those that a mesh axis runs over, the one named last changes fastest.
Arguments:
- query_rows: bfloat16 [16, 8192, 2048], P('dp', 'ctx'), may hold values from -72 to 72
- key_rows: bfloat16 [16, 8192, 512], P('dp', 'ctx'), may hold values from -4 to 4
- value_rows: bfloat16 [16, 8192, 512], P('dp', 'ctx'), may hold values from -6 to 6
- grad_rows: bfloat16 [16, 8192, 2048], P('dp', 'ctx'), may hold values from -6 to 6
- bucket_rank: int32 [16, 8192], P('dp', 'ctx'), may hold values from 0 to 255, as said below
- sample_rows: int32 [16, 64], P('dp', 'ctx'), may hold values from 0 to 127, as said below
- sample_count: int32 [16, 64], P('dp', 'ctx'), may hold values from 1 to 3
- sink_logit: float32 [16], replicated, may hold values from 3 to 6
Outputs:
- query_grad: bfloat16 [16, 8192, 2048], P('dp', 'ctx')
- key_grad: bfloat16 [16, 8192, 512], P('dp', 'ctx')
- value_grad: bfloat16 [16, 8192, 512], P('dp', 'ctx')
- sink_grad: float32 [16], replicated
Inputs may be any that keep to these rules, and one draw needn't show every extreme that they name: `bucket_rank`: for every sequence and every m, the values over the 256 tokens held by ctx indices 2m and 2m+1 are a permutation of 0 to 255. `sample_rows`: slot c names a row of the 128 tokens held by ctx index c, counted from that block's first token; the slots of one block name distinct rows.
All inputs are finite; a program needn't handle non-finite values.
Results may differ from a plain program's by a relative error of at most 0.0075.
Values may be sent and summed in bfloat16 or wider, within the bound.
A program may use at most 32 MiB of HBM per device.

v0:
```python
import jax
import jax.numpy as jnp
from jax import lax
from jax.sharding import PartitionSpec as P

HEADS = 16
KV_HEADS = 4
HDIM = 128
BUCKET = 128
SAMP_DEV = 1


def swapped(array, axis, apart):
    return lax.ppermute(array, axis, [(i, i ^ 1 << apart) for i in range(lax.axis_size(axis))])


def on_device(
    query_rows, key_rows, value_rows, grad_rows, bucket_rank, sample_rows, sample_count, sink_logit
):
    length = query_rows.shape[1]
    per_group = HEADS // KV_HEADS
    kv_width = KV_HEADS * HDIM
    score_scale = HDIM ** (-0.5)
    query_heads = query_rows[0].reshape(length, KV_HEADS, per_group, HDIM)
    grad_heads = grad_rows[0].reshape(length, KV_HEADS, per_group, HDIM)
    own_bucket = bucket_rank[0] // BUCKET
    own_mark = own_bucket.astype(jnp.bfloat16)
    far_keys, far_values, far_mark = swapped((key_rows[0], value_rows[0], own_mark), "ctx", 0)
    pair_keys = jnp.concatenate([key_rows[0], far_keys], 0).reshape(2 * length, KV_HEADS, HDIM)
    pair_values = jnp.concatenate([value_rows[0], far_values], 0).reshape(
        2 * length, KV_HEADS, HDIM
    )
    query_bucket = own_bucket.astype(jnp.float32)
    pair_bucket = jnp.concatenate([query_bucket, far_mark.astype(jnp.float32)], 0)
    picked = sample_rows[0]
    picked_keys = jnp.take(key_rows[0], picked, axis=0)
    picked_values = jnp.take(value_rows[0], picked, axis=0)
    picked_mark = jnp.take(own_mark, picked, axis=0)
    picked_count = sample_count[0].astype(jnp.bfloat16)
    panel_keys, panel_values, panel_mark, panel_count = (
        lax.all_gather(picked_keys, "ctx", axis=0, tiled=True),
        lax.all_gather(picked_values, "ctx", axis=0, tiled=True),
        lax.all_gather(picked_mark, "ctx", axis=0, tiled=True),
        lax.all_gather(picked_count, "ctx", axis=0, tiled=True),
    )
    samples = panel_keys.shape[0]
    sample_keys = panel_keys.reshape(samples, KV_HEADS, HDIM)
    sample_values = panel_values.reshape(samples, KV_HEADS, HDIM)
    owner_pair = jnp.arange(samples, dtype=jnp.int32) // SAMP_DEV // 2
    same_pair = owner_pair == lax.axis_index("ctx") // 2
    excluded = same_pair[None, :] & (
        query_bucket[:, None] == panel_mark.astype(jnp.float32)[None, :]
    )
    log_weight = jnp.log(panel_count.astype(jnp.float32))
    inside = query_bucket[:, None] == pair_bucket[None, :]
    bucket_score = (
        jnp.einsum("tkgd,jkd->tkgj", query_heads, pair_keys, preferred_element_type=jnp.float32)
        * score_scale
    )
    bucket_score = jnp.where(inside[:, None, None, :], bucket_score, -jnp.inf)
    sample_score = (
        jnp.einsum("tkgd,ckd->tkgc", query_heads, sample_keys, preferred_element_type=jnp.float32)
        * score_scale
        + log_weight
    )
    sample_score = jnp.where(excluded[:, None, None, :], -jnp.inf, sample_score)
    sink_row = sink_logit.reshape(KV_HEADS, per_group)
    row_max = jnp.maximum(
        jnp.maximum(jnp.max(bucket_score, -1), jnp.max(sample_score, -1)), sink_row
    )
    denominator = (
        jnp.exp(sink_row - row_max)
        + jnp.sum(jnp.exp(bucket_score - row_max[..., None]), -1)
        + jnp.sum(jnp.exp(sample_score - row_max[..., None]), -1)
    )
    log_total = row_max + jnp.log(denominator)
    bucket_prob = jnp.exp(bucket_score - log_total[..., None])
    sample_prob = jnp.exp(sample_score - log_total[..., None])
    sink_prob = jnp.exp(sink_row - log_total)
    bucket_half = bucket_prob.astype(jnp.bfloat16)
    sample_half = sample_prob.astype(jnp.bfloat16)
    attended = (
        jnp.einsum("tkgj,jkd->tkgd", bucket_half, pair_values, preferred_element_type=jnp.float32)
        + jnp.einsum(
            "tkgc,ckd->tkgd", sample_half, sample_values, preferred_element_type=jnp.float32
        )
    ).astype(jnp.bfloat16)
    delta = jnp.einsum("tkgd,tkgd->tkg", grad_heads, attended, preferred_element_type=jnp.float32)
    bucket_up = jnp.einsum(
        "tkgd,jkd->tkgj", grad_heads, pair_values, preferred_element_type=jnp.float32
    )
    sample_up = jnp.einsum(
        "tkgd,ckd->tkgc", grad_heads, sample_values, preferred_element_type=jnp.float32
    )
    bucket_ds = (bucket_prob * (bucket_up - delta[..., None])).astype(jnp.bfloat16)
    sample_ds = (sample_prob * (sample_up - delta[..., None])).astype(jnp.bfloat16)
    query_grad = score_scale * (
        jnp.einsum("tkgj,jkd->tkgd", bucket_ds, pair_keys, preferred_element_type=jnp.float32)
        + jnp.einsum("tkgc,ckd->tkgd", sample_ds, sample_keys, preferred_element_type=jnp.float32)
    )
    query_grad = query_grad.reshape(1, length, HEADS * HDIM).astype(jnp.bfloat16)
    key_pair_grad = score_scale * jnp.einsum(
        "tkgj,tkgd->jkd", bucket_ds, query_heads, preferred_element_type=jnp.float32
    )
    value_pair_grad = jnp.einsum(
        "tkgj,tkgd->jkd", bucket_half, grad_heads, preferred_element_type=jnp.float32
    )
    key_from_far, value_from_far = (
        swapped(key_pair_grad[length:].astype(jnp.bfloat16), "ctx", 0).astype(jnp.float32),
        swapped(value_pair_grad[length:].astype(jnp.bfloat16), "ctx", 0).astype(jnp.float32),
    )
    key_term = score_scale * jnp.einsum(
        "tkgc,tkgd->ckd", sample_ds, query_heads, preferred_element_type=jnp.float32
    )
    value_term = jnp.einsum(
        "tkgc,tkgd->ckd", sample_half, grad_heads, preferred_element_type=jnp.float32
    )
    own_slots = lax.psum_scatter(
        jnp.concatenate(
            [
                key_term.reshape(lax.axis_size("ctx") * SAMP_DEV, kv_width),
                value_term.reshape(lax.axis_size("ctx") * SAMP_DEV, kv_width),
            ],
            1,
        ),
        "ctx",
        scatter_dimension=0,
        tiled=True,
    )
    one_hot = (picked[:, None] == jnp.arange(length, dtype=jnp.int32)[None, :]).astype(jnp.float32)
    slot_rows = jnp.dot(
        one_hot.T, own_slots, preferred_element_type=jnp.float32, precision=lax.Precision.HIGHEST
    )
    key_grad = (
        key_pair_grad[:length].reshape(length, kv_width)
        + key_from_far.reshape(length, kv_width)
        + slot_rows[:, :kv_width]
    )
    value_grad = (
        value_pair_grad[:length].reshape(length, kv_width)
        + value_from_far.reshape(length, kv_width)
        + slot_rows[:, kv_width:]
    )
    sink_local = -jnp.sum(sink_prob * delta, 0).reshape(HEADS)
    sink_grad = lax.psum(sink_local, ("dp", "ctx"))
    return (
        query_grad,
        key_grad.reshape(1, length, kv_width).astype(jnp.bfloat16),
        value_grad.reshape(1, length, kv_width).astype(jnp.bfloat16),
        sink_grad,
    )


def solution(mesh):
    return jax.shard_map(
        on_device,
        mesh=mesh,
        in_specs=(
            P("dp", "ctx", None),
            P("dp", "ctx", None),
            P("dp", "ctx", None),
            P("dp", "ctx", None),
            P("dp", "ctx"),
            P("dp", "ctx"),
            P("dp", "ctx"),
            P(),
        ),
        out_specs=(P("dp", "ctx", None), P("dp", "ctx", None), P("dp", "ctx", None), P()),
        check_vma=False,
    )
```

profile of v0, /device:TPU:4, one launch (start us, length us, event | category | flops | bytes accessed | tf_op | source)
XLA Modules:
  0.0 472.4 jit_solution(9670105795213841515)
XLA Ops:
  7.2 0.0 all-reduce.6.cloned.1.call-start
  7.2 0.7 fusion.43
  7.9 3.4 collective-permute-start.1
  11.3 1.0 copy.86
  12.3 2.4 collective-permute-start
  14.8 1.0 copy.93
  15.8 3.5 collective-permute-start.2
  20.0 0.5 compare_select_fusion
  20.5 1.2 dynamic-slice_select_fusion
  21.8 1.5 select_reduce_fusion.1
  23.3 1.5 select_reduce_fusion
  25.4 1.4 fusion.44
  26.9 1.4 dynamic-update-slice.2
  28.3 0.8 dynamic-update-slice.3
  29.0 147.0 %all-reduce.3 = (bf16[64]{0:T(256)(128)(2,1)S(1)}, bf16[64]{0:T(256)(128)(2,1)S(1)}) all-reduce(bf16[64]{0:T(256)(128)(2,1)S(1)} %dynamic-update-slice.3, bf16[64]{0:T(256)(128)(2,1)S(1)} %dynamic-update-slice.2), channel_id=2, replica_groups=mesh['dp'=16,'ctx'=64] {'ctx'}, use_global_device_ids=true, to_apply=%add.1 | all-reduce | flops 128 | bytes 512
  176.1 49.0 %all-gather.1 = bf16[64,1,512]{2,1,0:T(2,128)(2,1)S(1)} all-gather(bf16[1,1,512]{2,1,0:T(2,128)(2,1)S(1)} %reshape.296), channel_id=1, replica_groups=mesh['dp'=16,'ctx'=64] {'ctx'}, dimensions={0}, use_global_device_ids=true | all-gather | bytes 66560 | tf_op jit(solution)/shard_map/all_gather | solution.py:41
  225.1 0.4 reduce.2
  225.5 1.4 reshape_squeeze.6
  226.9 0.0 copy-start.1
  226.9 0.8 copy.88
  227.7 0.1 max.28
  227.8 0.1 copy.95
  228.0 47.7 %all-gather.2 = bf16[64,1,512]{2,1,0:T(2,128)(2,1)S(1)} all-gather(bf16[1,1,512]{2,1,0:T(2,128)(2,1)S(1)} %reshape.298), channel_id=1, replica_groups=mesh['dp'=16,'ctx'=64] {'ctx'}, dimensions={0}, use_global_device_ids=true | all-gather | bytes 66560 | tf_op jit(solution)/shard_map/all_gather | solution.py:42
  275.6 0.5 fusion.38
  276.1 0.1 compare_and_fusion
  276.2 0.9 fusion.46
  277.2 0.4 reduce.4
  277.6 0.4 reshape_squeeze.7
  277.9 0.5 copy.114
  278.4 0.7 broadcast_compare_fusion
  279.2 0.8 copy.89
  279.9 1.6 fusion.45
  281.6 0.8 maximum_maximum_fusion
  282.4 0.9 exponential_reduce_fusion
  283.3 0.7 exponential_reduce_fusion.1
  284.0 1.0 copy.96
  285.0 0.8 log_add_fusion
  285.8 0.5 fusion.24
  286.3 1.4 fusion.7
  287.7 2.6 copy.126
  290.3 2.8 multiply_reduce_fusion
  293.1 1.0 copy.127
  294.1 0.6 fusion.1
  294.7 0.2 fusion.15
  294.9 0.3 convolution_bitcast_fusion.3
  295.2 1.3 convolution_bitcast_fusion
  296.5 0.2 multiply_reduce_fusion.1
  296.7 0.5 fusion.14
  297.2 0.3 fusion.28
  297.6 1.9 collective-permute-start.3
  299.5 0.2 fusion.17
  299.8 0.7 pad_maximum_fusion
  300.5 0.0 all-reduce.6.cloned.1.call-update
  300.6 3.9 collective-permute-start.4
  304.5 0.1 neg.7
  304.6 0.3 fusion.5
  305.0 116.3 %psum.7 = f32[16]{0:T(128)} all-reduce(f32[16]{0:T(128)S(1)} %neg.7), channel_id=1, replica_groups=mesh['dp'=16,'ctx'=64] {'dp','ctx'}, use_global_device_ids=true, to_apply=%region_6.8 | all-reduce | flops 16 | bytes 128 | tf_op jit(solution)/shard_map/psum | solution.py:145
  421.3 1.0 copy.116
  422.3 0.1 copy.112
  422.5 0.1 copy.115
  422.6 40.6 %all-reduce.6.cloned.1.call-done = f32[64,1024]{1,0:T(8,128)} async-done(((f32[64,1024]{1,0:T(8,128)}), f32[64,1024]{1,0:T(8,128)}) %all-reduce.6.cloned.1.call-update) | async-done | bytes 262160
  463.3 1.4 constant_dynamic-slice_fusion
  464.7 0.1 broadcast_multiply_fusion
  464.8 0.8 fusion.30
  (45 shorter events, 0.3 us)
Async XLA Ops:
  7.2 220.6 %copy-start.10 = (f32[16]{0:T(128)S(1)}, f32[16]{0:T(128)}, u32[]{:S(2)}) copy-start(f32[16]{0:T(128)} %param.17) | copy-start | bytes 196
  7.2 456.1 %all-reduce.6.cloned.1.call-start = ((), (), s32[]{:S(2)}) async-start(), calls=%async_computation | async-start | bytes 524288
  7.9 270.5 %collective-permute-start.1 = (bf16[128]{0:T(256)(128)(2,1)S(1)}, bf16[128]{0:T(256)(128)(2,1)S(1)}, u32[]{:S(2)}, u32[]{:S(2)}) collective-permute-start(bf16[128]{0:T(256)(128)(2,1)S(1)} %get-tuple-element.45), channel_id=1, source_target_pairs={{0,1},{1,0},{2,3},{3,2},{4,5},{5,4},{6,7},{7,6},{8,9},{9,8},{10,11... | collective-permute-start | bytes 776 | tf_op jit(solution)/shard_map/ppermute | solution.py:14
  12.3 266.8 %collective-permute-start = (bf16[128,512]{0,1:T(8,128)(2,1)S(1)}, bf16[128,512]{0,1:T(8,128)(2,1)S(1)}, u32[]{:S(2)}, u32[]{:S(2)}) collective-permute-start(bf16[128,512]{0,1:T(8,128)(2,1)S(1)} %bitcast.137), channel_id=1, source_target_pairs={{0,1},{1,0},{2,3},{3,2},{4,5},{5,4},{6,7},{7,6},{8,9},{9,8},{10,11... | collective-permute-start | bytes 393224 | tf_op jit(solution)/shard_map/ppermute | solution.py:14
  15.8 261.8 %copy-start.6 = (bf16[1,128,2048]{2,1,0:T(8,128)(2,1)S(1)}, bf16[1,128,2048]{2,1,0:T(8,128)(2,1)}, u32[]{:S(2)}) copy-start(bf16[1,128,2048]{2,1,0:T(8,128)(2,1)} %param.13) | copy-start | bytes 1572868
  15.8 268.2 %collective-permute-start.2 = (bf16[128,512]{0,1:T(8,128)(2,1)S(1)}, bf16[128,512]{0,1:T(8,128)(2,1)}, u32[]{:S(2)}, u32[]{:S(2)}) collective-permute-start(bf16[128,512]{0,1:T(8,128)(2,1)S(1)} %bitcast.134), channel_id=1, source_target_pairs={{0,1},{1,0},{2,3},{3,2},{4,5},{5,4},{6,7},{7,6},{8,9},{9,8},{10,11... | collective-permute-start | bytes 393224 | tf_op jit(solution)/shard_map/ppermute | solution.py:14
  226.9 50.7 %copy-start.1 = (bf16[128,4,4,128]{3,2,1,0:T(4,128)(2,1)}, bf16[128,4,4,128]{3,2,1,0:T(4,128)(2,1)S(1)}, u32[]{:S(2)}) copy-start(bf16[128,4,4,128]{3,2,1,0:T(4,128)(2,1)S(1)} %reshape_squeeze.6) | copy-start | bytes 1572868
  227.8 53.8 %copy-start.7 = (f32[4,4]{1,0:T(4,128)}, f32[4,4]{1,0:T(4,128)S(1)}, u32[]{:S(2)}) copy-start(f32[4,4]{1,0:T(4,128)S(1)} %max.28) | copy-start | bytes 196
  277.9 1.2 copy-start
  294.9 1.6 copy-start.8
  294.9 1.8 copy-start.2
  295.2 2.0 copy-start.4
  295.2 2.0 copy-start.5
  297.2 3.4 copy-start.3
  297.6 124.7 %collective-permute-start.3 = (bf16[128,4,128]{0,2,1:T(8,128)(2,1)S(1)}, bf16[128,4,128]{0,2,1:T(8,128)(2,1)S(1)}, u32[]{:S(2)}, u32[]{:S(2)}) collective-permute-start(bf16[128,4,128]{0,2,1:T(8,128)(2,1)S(1)} %slice.59), channel_id=1, source_target_pairs={{0,1},{1,0},{2,3},{3,2},{4,5},{5,4},{6,7},{7,6},{8,9},{9,8},{10,11... | collective-permute-start | bytes 393224 | tf_op jit(solution)/shard_map/ppermute | solution.py:14
  300.6 121.8 %collective-permute-start.4 = (bf16[128,4,128]{0,2,1:T(8,128)(2,1)S(1)}, bf16[128,4,128]{0,2,1:T(8,128)(2,1)S(1)}, u32[]{:S(2)}, u32[]{:S(2)}) collective-permute-start(bf16[128,4,128]{0,2,1:T(8,128)(2,1)S(1)} %slice.58), channel_id=1, source_target_pairs={{0,1},{1,0},{2,3},{3,2},{4,5},{5,4},{6,7},{7,6},{8,9},{9,8},{10,11... | collective-permute-start | bytes 393224 | tf_op jit(solution)/shard_map/ppermute | solution.py:14
  305.0 159.7 %copy-start.9 = (f32[128]{0:T(128)S(1)}, f32[128]{0:T(128)}, u32[]{:S(2)}) copy-start(f32[128]{0:T(128)} %fusion.38) | copy-start | bytes 1540
Sparse Core Ops, SparseCore 0:
  300.7 162.5 all-reduce.5
where the time goes:
time: 473 us; the launch traced here: 472 us
  blocking collectives  360 us (76%)
  waiting for transfers between devices  40.7 us (9%)
  local copies, waits for them, and re-layouts  17.3 us (4%)
  between operations  15.8 us (3%)
  other arithmetic  15.3 us (3%)
  starting transfers between devices  15.2 us (3%)
  matrix products  8.2 us (2%)
    unnamed x1, blocking collectives  147 us
    psum x1, blocking collectives, on_device(): sink_grad = lax.psum(sink_local, ('dp', 'ctx'))  116 us
    all_gather x1, blocking collectives, on_device(): lax.all_gather(picked_keys, 'ctx', axis=0, tiled=True)  49 us
    all_gather x1, blocking collectives, on_device(): lax.all_gather(picked_values, 'ctx', axis=0, tiled=True)  47.7 us
    unnamed x2, waiting for transfers between devices  40.7 us
    ppermute x5, starting transfers between devices, swapped(): lax.ppermute(array, axis, [(i, i ^ 1 << apart) for i in range(lax.axis_si...  15.2 us
    unnamed x34, local copies, waits for them, and re-layouts  10.7 us
  transfers between devices with their start and end apart: 6, of which 1 were waited for; matrix products, arithmetic and copies ran while one was open for 5% of the time, Pallas kernels for 0%

commit v1 on v0

v1 whole, which is shorter than its diff:
```python
import functools

import jax
import jax.numpy as jnp
from jax import lax
from jax.experimental import pallas as pl
from jax.experimental.pallas import tpu as pltpu
from jax.sharding import PartitionSpec as P

HEADS = 16
KV_HEADS = 4
HDIM = 128
BUCKET = 128
GROUP = HEADS // KV_HEADS
WIDTH = KV_HEADS * HDIM
ROW = 2 * WIDTH + 128
NEG = -1e30
MESH = pl.DeviceIdType.MESH


def whole_kernel(
    ny, nx, ndp,
    q_ref, k_ref, v_ref, g_ref, rank_ref, rows_ref, count_ref, sink_ref,
    dq_ref, dk_ref, dv_ref, ds_ref,
    row_buf, rows1, blk_buf, samples, far_k, far_v, far_rank,
    prob, dscore, own_k, own_v, back_buf, back, terms, terms_in, lines, lines_in,
    sink_buf, sink_dp, sink_part, sink_y,
    x_send, x_recv, y_send, y_recv, pair_send, pair_recv,
    back_send, back_recv, t_send, t_recv, l_send, l_recv,
    sd_send, sd_recv, sy_send, sy_recv,
):
    f32, bf16 = jnp.float32, jnp.bfloat16
    length = k_ref.shape[0]
    slots = ny * nx
    keys = 2 * length + slots
    scale = HDIM ** (-0.5)
    ctx, dp = lax.axis_index("ctx"), lax.axis_index("dp")
    y, x = ctx // nx, ctx % nx

    def x_peer(d):
        return {"ctx": y * nx + (x + d) % nx}

    def y_peer(d):
        return {"ctx": ((y + d) % ny) * nx + x}

    def dp_peer(d):
        return {"dp": (dp + d) % ndp}

    partner = {"ctx": y * nx + x + 1 - 2 * (x % 2)}
    started = []

    def send(src, dst, ssem, rsem, device):
        copy = pltpu.make_async_remote_copy(
            src_ref=src, dst_ref=dst, send_sem=ssem, recv_sem=rsem,
            device_id=device, device_id_type=MESH,
        )
        copy.start()
        started.append(copy)
        return copy

    barrier = pltpu.get_barrier_semaphore()
    peers = (
        [x_peer(d) for d in range(1, nx)]
        + [y_peer(d) for d in range(1, ny)]
        + [dp_peer(d) for d in range(1, ndp)]
    )
    for peer in peers:
        pl.semaphore_signal(barrier, inc=1, device_id=peer, device_id_type=MESH)

    lane = lax.broadcasted_iota(jnp.int32, (8, length), 1)
    picked = rows_ref[...]
    hit = lane == picked
    one_hot = jnp.where(hit, 1.0, 0.0).astype(bf16)
    own_row = rank_ref[...]
    own_bucket = jnp.where(own_row >= BUCKET, 1.0, 0.0)
    mark = jnp.sum(jnp.where(hit, own_bucket, 0.0), axis=1, keepdims=True)
    row_buf[:, :WIDTH] = jnp.dot(one_hot, k_ref[...], preferred_element_type=f32)
    row_buf[:, WIDTH : 2 * WIDTH] = jnp.dot(one_hot, v_ref[...], preferred_element_type=f32)
    tail = lax.broadcasted_iota(jnp.int32, (8, 128), 1)
    row_buf[:, 2 * WIDTH :] = jnp.where(
        tail == 0, count_ref[...].astype(f32), jnp.where(tail == 1, mark, 0.0)
    )
    rows1[pl.ds(x, 1), :] = row_buf[0:1, :]
    pl.semaphore_wait(barrier, len(peers))

    x_copies = [
        send(row_buf.at[pl.ds(0, 1)], rows1.at[pl.ds(x, 1)],
             x_send.at[d - 1], x_recv.at[d - 1], x_peer(d))
        for d in range(1, nx)
    ]
    pair_copies = [
        send(rank_ref, far_rank, pair_send.at[0], pair_recv.at[0], partner),
        send(k_ref, far_k, pair_send.at[1], pair_recv.at[1], partner),
        send(v_ref, far_v, pair_send.at[2], pair_recv.at[2], partner),
    ]
    for copy in x_copies:
        copy.wait_recv()
    blk_buf[...] = rows1[...].astype(bf16)
    samples[y] = rows1[...].astype(bf16)
    y_copies = [
        send(blk_buf, samples.at[y], y_send.at[d - 1], y_recv.at[d - 1], y_peer(d))
        for d in range(1, ny)
    ]
    for copy in pair_copies:
        copy.wait_recv()
    for copy in y_copies:
        copy.wait_recv()

    panel = jnp.concatenate([samples[i].astype(f32) for i in range(ny)], 0)
    panel_kv = panel[:, : 2 * WIDTH].astype(bf16)
    counts = panel[:, 2 * WIDTH : 2 * WIDTH + 1]
    marks = panel[:, 2 * WIDTH + 1 : 2 * WIDTH + 2]
    up = lax.broadcasted_iota(jnp.int32, (length, length), 0)
    across = lax.broadcasted_iota(jnp.int32, (length, length), 1)
    far_bucket = jnp.where(far_rank[...] >= BUCKET, 1.0, 0.0)

    def upright(line):
        return jnp.sum(jnp.where(up == across, line, 0.0), axis=1, keepdims=True)

    key_bucket = jnp.concatenate([upright(own_bucket), upright(far_bucket)], 0)
    slot = lax.broadcasted_iota(jnp.int32, (slots, 1), 0)
    near = jnp.where(slot // 2 == ctx // 2, marks, 2.0)
    bias = jnp.concatenate(
        [
            jnp.where(key_bucket == own_bucket, 0.0, NEG),
            jnp.where(near == own_bucket, NEG, jnp.log(counts)),
        ],
        0,
    )
    bias = jnp.concatenate([bias] * GROUP, 1)

    def heads_of(ref, j):
        first = j * GROUP * HDIM
        return jnp.concatenate(
            [ref[:, first + h * HDIM : first + (h + 1) * HDIM] for h in range(GROUP)], 0
        )

    def keys_of(own, far, offset, j):
        cut = slice(j * HDIM, (j + 1) * HDIM)
        return jnp.concatenate(
            [own[:, cut], far[:, cut], panel_kv[:, offset + j * HDIM : offset + (j + 1) * HDIM]], 0
        )

    transposed = (((1,), (1,)), ((), ()))
    sink_lane = lax.broadcasted_iota(jnp.int32, (1, 128), 1)
    sink_line = jnp.zeros((1, 128), f32)
    for j in range(KV_HEADS):
        score = lax.dot_general(
            keys_of(k_ref, far_k, 0, j), heads_of(q_ref, j), transposed,
            preferred_element_type=f32,
        ) * scale + bias
        sink_row = jnp.concatenate(
            [jnp.full((1, length), sink_ref[j * GROUP + h], f32) for h in range(GROUP)], 1
        )
        top = jnp.maximum(jnp.max(score, axis=0, keepdims=True), sink_row)
        weight = jnp.exp(score - top)
        sink_weight = jnp.exp(sink_row - top)
        inverse = 1.0 / (jnp.sum(weight, axis=0, keepdims=True) + sink_weight)
        chance = weight * inverse
        lift = lax.dot_general(
            keys_of(v_ref, far_v, WIDTH, j), heads_of(g_ref, j), transposed,
            preferred_element_type=f32,
        )
        delta = jnp.sum(chance * lift, axis=0, keepdims=True)
        prob[j] = chance.astype(bf16)
        dscore[j] = (chance * (lift - delta)).astype(bf16)
        sink_term = sink_weight * inverse * delta
        for h in range(GROUP):
            part = jnp.sum(sink_term[:, h * length : (h + 1) * length], axis=1, keepdims=True)
            sink_line = jnp.where(sink_lane == j * GROUP + h, part, sink_line)
    sink_buf[...] = sink_line
    sink_dp[pl.ds(dp, 1), :] = sink_line
    dp_copies = [
        send(sink_buf, sink_dp.at[pl.ds(dp, 1)], sd_send.at[d - 1], sd_recv.at[d - 1], dp_peer(d))
        for d in range(1, ndp)
    ]

    t_copies, back_copies = [], []
    for j in range(KV_HEADS):
        cut = slice(j * HDIM, (j + 1) * HDIM)
        ds_t, p_t = dscore[j], prob[j]
        q_part, g_part = heads_of(q_ref, j), heads_of(g_ref, j)
        key_all = jnp.dot(ds_t, q_part, preferred_element_type=f32) * scale
        value_all = jnp.dot(p_t, g_part, preferred_element_type=f32)
        for i in range(ny):
            low = 2 * length + i * nx
            terms[j, i, :, :HDIM] = key_all[low : low + nx].astype(bf16)
            terms[j, i, :, HDIM:] = value_all[low : low + nx].astype(bf16)
        terms_in[j, y] = terms[j, y]
        for d in range(1, ny):
            t_copies.append(send(
                terms.at[j, (y + d) % ny], terms_in.at[j, y],
                t_send.at[j, d - 1], t_recv.at[j, d - 1], y_peer(d),
            ))
        back_buf[j, :, :HDIM] = key_all[length : 2 * length].astype(bf16)
        back_buf[j, :, HDIM:] = value_all[length : 2 * length].astype(bf16)
        back_copies.append(send(
            back_buf.at[j], back.at[j], back_send.at[j], back_recv.at[j], partner
        ))
        own_k[:, cut] = key_all[:length]
        own_v[:, cut] = value_all[:length]
    for copy in dp_copies:
        copy.wait_recv()
    sink_sum = jnp.sum(sink_dp[...], axis=0, keepdims=True)
    sink_part[...] = sink_sum
    sink_y[pl.ds(y, 1), :] = sink_sum
    sy_copies = [
        send(sink_part, sink_y.at[pl.ds(y, 1)], sy_send.at[d - 1], sy_recv.at[d - 1], y_peer(d))
        for d in range(1, ny)
    ]
    for j in range(KV_HEADS):
        query_part = scale * lax.dot_general(
            dscore[j], keys_of(k_ref, far_k, 0, j), (((0,), (0,)), ((), ())),
            preferred_element_type=f32,
        )
        for h in range(GROUP):
            first = (j * GROUP + h) * HDIM
            dq_ref[:, first : first + HDIM] = query_part[h * length : (h + 1) * length].astype(bf16)
    for copy in t_copies:
        copy.wait_recv()
    for copy in sy_copies:
        copy.wait_recv()
    for j in range(KV_HEADS):
        total = terms_in[j, 0].astype(f32)
        for i in range(1, ny):
            total = total + terms_in[j, i].astype(f32)
        lines[:, j * HDIM : (j + 1) * HDIM] = total[:, :HDIM]
        lines[:, WIDTH + j * HDIM : WIDTH + (j + 1) * HDIM] = total[:, HDIM:]
    lines[:, 2 * WIDTH :] = jnp.broadcast_to(
        jnp.sum(sink_y[...], axis=0, keepdims=True), (nx, 128)
    )
    lines_in[pl.ds(x, 1), :] = lines[pl.ds(x, 1), :]
    l_copies = [
        send(lines.at[pl.ds((x + d) % nx, 1)], lines_in.at[pl.ds(x, 1)],
             l_send.at[d - 1], l_recv.at[d - 1], x_peer(d))
        for d in range(1, nx)
    ]
    for copy in back_copies:
        copy.wait_recv()
    for copy in l_copies:
        copy.wait_recv()
    line = jnp.sum(lines_in[...], axis=0, keepdims=True)
    here = lax.broadcasted_iota(jnp.int32, (length, HDIM), 0) == picked
    for j in range(KV_HEADS):
        cut = slice(j * HDIM, (j + 1) * HDIM)
        dk_ref[:, cut] = (
            own_k[:, cut] + back[j, :, :HDIM].astype(f32) + jnp.where(here, line[:, cut], 0.0)
        ).astype(bf16)
        dv_ref[:, cut] = (
            own_v[:, cut]
            + back[j, :, HDIM:].astype(f32)
            + jnp.where(here, line[:, WIDTH + j * HDIM : WIDTH + (j + 1) * HDIM], 0.0)
        ).astype(bf16)
    ds_ref[...] = -line[:, 2 * WIDTH :]
    for copy in started:
        copy.wait_send()


def on_device(
    ndp, query_rows, key_rows, value_rows, grad_rows, bucket_rank, sample_rows, sample_count, sink_logit
):
    length = query_rows.shape[1]
    slots = lax.axis_size("ctx")
    nx = 8 if slots >= 64 else 2
    ny = slots // nx
    keys = 2 * length + slots
    f32, bf16, i32 = jnp.float32, jnp.bfloat16, jnp.int32
    vmem, dma = pltpu.VMEM, pltpu.SemaphoreType.DMA
    space = pl.BlockSpec(memory_space=pltpu.VMEM)
    dq, dk, dv, ds = pl.pallas_call(
        functools.partial(whole_kernel, ny, nx, ndp),
        out_shape=[
            jax.ShapeDtypeStruct((length, HEADS * HDIM), bf16),
            jax.ShapeDtypeStruct((length, WIDTH), bf16),
            jax.ShapeDtypeStruct((length, WIDTH), bf16),
            jax.ShapeDtypeStruct((1, 128), f32),
        ],
        in_specs=[space] * 7 + [pl.BlockSpec(memory_space=pltpu.SMEM)],
        out_specs=[space] * 4,
        scratch_shapes=[
            vmem((8, ROW), f32),
            vmem((nx, ROW), f32),
            vmem((nx, ROW), bf16),
            vmem((ny, nx, ROW), bf16),
            vmem((length, WIDTH), bf16),
            vmem((length, WIDTH), bf16),
            vmem((1, length), i32),
            vmem((KV_HEADS, keys, GROUP * length), bf16),
            vmem((KV_HEADS, keys, GROUP * length), bf16),
            vmem((length, WIDTH), f32),
            vmem((length, WIDTH), f32),
            vmem((KV_HEADS, length, 2 * HDIM), bf16),
            vmem((KV_HEADS, length, 2 * HDIM), bf16),
            vmem((KV_HEADS, ny, nx, 2 * HDIM), bf16),
            vmem((KV_HEADS, ny, nx, 2 * HDIM), bf16),
            vmem((nx, ROW), f32),
            vmem((nx, ROW), f32),
            vmem((1, 128), f32),
            vmem((ndp, 128), f32),
            vmem((1, 128), f32),
            vmem((ny, 128), f32),
            dma((nx - 1,)), dma((nx - 1,)),
            dma((ny - 1,)), dma((ny - 1,)),
            dma((3,)), dma((3,)),
            dma((KV_HEADS,)), dma((KV_HEADS,)),
            dma((KV_HEADS, ny - 1)), dma((KV_HEADS, ny - 1)),
            dma((nx - 1,)), dma((nx - 1,)),
            dma((ndp - 1,)), dma((ndp - 1,)),
            dma((ny - 1,)), dma((ny - 1,)),
        ],
        compiler_params=pltpu.CompilerParams(
            collective_id=0, has_side_effects=True, vmem_limit_bytes=40 << 20
        ),
    )(
        query_rows[0], key_rows[0], value_rows[0], grad_rows[0],
        bucket_rank, sample_rows, sample_count, sink_logit,
    )
    return dq[None], dk[None], dv[None], ds[0, :HEADS]


def solution(mesh):
    return jax.shard_map(
        functools.partial(on_device, mesh.shape["dp"]),
        mesh=mesh,
        in_specs=(
            P("dp", "ctx", None),
            P("dp", "ctx", None),
            P("dp", "ctx", None),
            P("dp", "ctx", None),
            P("dp", "ctx"),
            P("dp", "ctx"),
            P("dp", "ctx"),
            P(),
        ),
        out_specs=(P("dp", "ctx", None), P("dp", "ctx", None), P("dp", "ctx", None), P()),
        check_vma=False,
    )
```

time: 473 us -> 57.9 us (0.12)
  the two profiles are of different devices: /device:TPU:4 before, /device:TPU:8 now
where the time goes in v1:
time: 57.9 us; the launch traced here: 57.6 us
  Pallas kernels  48.5 us (84%)
  local copies, waits for them, and re-layouts  7.16 us (12%)
  between operations  1.96 us (3%)
    pallas_call x1, Pallas kernels, on_device(): pl.pallas_call(functools.partial(whole_kernel, ny, nx, ndp), out_shape=[j...  48.5 us
    unnamed x15, local copies, waits for them, and re-layouts  6.65 us

profile of v1, /device:TPU:8, one launch (start us, length us, event | category | flops | bytes accessed | tf_op | source)
XLA Modules:
  0.0 57.6 jit_solution(8394203033283672176)
XLA Ops:
  1.9 0.0 copy-start.4
  1.9 0.0 copy-start.5
  1.9 0.6 %copy-done.4 = s32[1,128]{1,0:T(1,128)S(1)} copy-done((s32[1,128]{1,0:T(1,128)S(1)}, s32[1,128]{1,0:T(1,128)}, u32[]{:S(2)}) %copy-start.4) | copy-done | bytes 536
  2.6 0.0 copy-done.5
  2.6 0.0 copy-start
  2.6 1.0 %copy-done = bf16[1,128,2048]{2,1,0:T(8,128)(2,1)S(1)} copy-done((bf16[1,128,2048]{2,1,0:T(8,128)(2,1)S(1)}, bf16[1,128,2048]{2,1,0:T(8,128)(2,1)}, u32[]{:S(2)}) %copy-start) | copy-done | bytes 524312
  3.6 0.0 copy-start.1
  3.6 1.0 %copy-done.1 = bf16[1,128,2048]{2,1,0:T(8,128)(2,1)S(1)} copy-done((bf16[1,128,2048]{2,1,0:T(8,128)(2,1)S(1)}, bf16[1,128,2048]{2,1,0:T(8,128)(2,1)}, u32[]{:S(2)}) %copy-start.1) | copy-done | bytes 524312
  4.7 0.0 copy-start.2
  4.7 0.9 %copy-done.2 = bf16[1,128,512]{2,1,0:T(8,128)(2,1)S(1)} copy-done((bf16[1,128,512]{2,1,0:T(8,128)(2,1)S(1)}, bf16[1,128,512]{2,1,0:T(8,128)(2,1)}, u32[]{:S(2)}) %copy-start.2) | copy-done | bytes 131096
  5.6 0.0 copy-start.3
  5.6 0.9 %copy-done.3 = bf16[1,128,512]{2,1,0:T(8,128)(2,1)S(1)} copy-done((bf16[1,128,512]{2,1,0:T(8,128)(2,1)S(1)}, bf16[1,128,512]{2,1,0:T(8,128)(2,1)}, u32[]{:S(2)}) %copy-start.3) | copy-done | bytes 131096
  6.5 48.5 %shard_map.111 = (bf16[128,2048]{1,0:T(8,128)(2,1)S(1)}, bf16[128,512]{1,0:T(8,128)(2,1)S(1)}, bf16[128,512]{1,0:T(8,128)(2,1)S(1)}, f32[1,128]{1,0:T(1,128)S(1)}) custom-call(bf16[128,2048]{1,0:T(8,128)(2,1)S(1)} %bitcast.9, bf16[128,512]{1,0:T(8,128)(2,1)S(1)} %bitcast.12, bf16[128,512]{1,0:T(8,128)(2,1)S(1)} %bitcast.13, bf16[128,2048]{1,0:T(8,128)(2,1)S(1)} %bitcast.10, ...), custom_call_target="tpu_custom_call" | custom-call | tf_op jit(solution)/shard_map/pallas_call | solution.py:270
  55.0 0.5 slice_bitcast_fusion
  55.5 0.8 %copy.17 = bf16[1,128,2048]{2,1,0:T(8,128)(2,1)} copy(bf16[1,128,2048]{2,1,0:T(8,128)(2,1)S(1)} %bitcast.11) | data formatting | bytes 1048576
  56.3 0.7 %copy.18 = bf16[1,128,512]{2,1,0:T(8,128)(2,1)} copy(bf16[1,128,512]{2,1,0:T(8,128)(2,1)S(1)} %bitcast.15) | data formatting | bytes 262144
  57.0 0.7 %copy.19 = bf16[1,128,512]{2,1,0:T(8,128)(2,1)} copy(bf16[1,128,512]{2,1,0:T(8,128)(2,1)S(1)} %bitcast.14) | data formatting | bytes 262144
Async XLA Ops:
  1.9 0.7 %copy-start.4 = (s32[1,128]{1,0:T(1,128)S(1)}, s32[1,128]{1,0:T(1,128)}, u32[]{:S(2)}) copy-start(s32[1,128]{1,0:T(1,128)} %rank_ref.1) | copy-start | bytes 1540
  1.9 0.7 %copy-start.5 = (f32[16]{0:T(128)S(1)}, f32[16]{0:T(128)}, u32[]{:S(2)}) copy-start(f32[16]{0:T(128)} %sink_ref.1) | copy-start | bytes 196
  2.6 1.0 %copy-start = (bf16[1,128,2048]{2,1,0:T(8,128)(2,1)S(1)}, bf16[1,128,2048]{2,1,0:T(8,128)(2,1)}, u32[]{:S(2)}) copy-start(bf16[1,128,2048]{2,1,0:T(8,128)(2,1)} %param.8) | copy-start | bytes 1572868
  3.6 1.0 %copy-start.1 = (bf16[1,128,2048]{2,1,0:T(8,128)(2,1)S(1)}, bf16[1,128,2048]{2,1,0:T(8,128)(2,1)}, u32[]{:S(2)}) copy-start(bf16[1,128,2048]{2,1,0:T(8,128)(2,1)} %param.11) | copy-start | bytes 1572868
  4.7 0.9 %copy-start.2 = (bf16[1,128,512]{2,1,0:T(8,128)(2,1)S(1)}, bf16[1,128,512]{2,1,0:T(8,128)(2,1)}, u32[]{:S(2)}) copy-start(bf16[1,128,512]{2,1,0:T(8,128)(2,1)} %param.9) | copy-start | bytes 393220
  5.6 0.9 %copy-start.3 = (bf16[1,128,512]{2,1,0:T(8,128)(2,1)S(1)}, bf16[1,128,512]{2,1,0:T(8,128)(2,1)}, u32[]{:S(2)}) copy-start(bf16[1,128,512]{2,1,0:T(8,128)(2,1)} %param.10) | copy-start | bytes 393220

commit v2 on v1

v2 whole, which is shorter than its diff:
```python
import functools

import jax
import jax.numpy as jnp
from jax import lax
from jax.experimental import pallas as pl
from jax.experimental.pallas import tpu as pltpu
from jax.sharding import PartitionSpec as P

HEADS = 16
KV_HEADS = 4
HDIM = 128
BUCKET = 128
GROUP = HEADS // KV_HEADS
WIDTH = KV_HEADS * HDIM
ROW = 2 * WIDTH + 128
NEG = -1e30
EARLY = 1
MESH = pl.DeviceIdType.MESH


def whole_kernel(
    ny, nx, ndp,
    q_hbm, k_hbm, v_hbm, g_hbm, rank_hbm, rows_hbm, count_hbm, sink_hbm,
    dq_ref, dk_ref, dv_ref, ds_ref,
    q_ref, k_ref, v_ref, g_ref, rank_ref, rows_ref, count_ref, sink_ref,
    row_buf, rows1, blk_buf, samples, far_k, far_v, far_rank,
    weights, lifts, stats, dscore, own_k, own_v, back_buf, back,
    terms, terms_in, lines, lines_in,
    sink_buf, sink_dp, sink_part, sink_y, sink_last, sink_x,
    in_sem, x_send, x_recv, y_send, y_recv, pair_send, pair_recv,
    back_send, back_recv, t_send, t_recv, l_send, l_recv,
    sd_send, sd_recv, sy_send, sy_recv, sx_send, sx_recv,
):
    f32, bf16 = jnp.float32, jnp.bfloat16
    length = k_ref.shape[0]
    slots = ny * nx
    scale = HDIM ** (-0.5)
    ctx, dp = lax.axis_index("ctx"), lax.axis_index("dp")
    y, x = ctx // nx, ctx % nx

    def x_peer(d):
        return {"ctx": y * nx + (x + d) % nx}

    def y_peer(d):
        return {"ctx": ((y + d) % ny) * nx + x}

    def dp_peer(d):
        return {"dp": (dp + d) % ndp}

    partner = {"ctx": y * nx + x + 1 - 2 * (x % 2)}
    started = []

    def send(src, dst, ssem, rsem, device):
        copy = pltpu.make_async_remote_copy(
            src_ref=src, dst_ref=dst, send_sem=ssem, recv_sem=rsem,
            device_id=device, device_id_type=MESH,
        )
        copy.start()
        started.append(copy)
        return copy

    def arrived(copies):
        for copy in copies:
            copy.wait_recv()

    barrier = pltpu.get_barrier_semaphore()
    peers = (
        [x_peer(d) for d in range(1, nx)]
        + [y_peer(d) for d in range(1, ny)]
        + [dp_peer(d) for d in range(1, ndp)]
    )
    for peer in peers:
        pl.semaphore_signal(barrier, inc=1, device_id=peer, device_id_type=MESH)
    loads = [
        pltpu.make_async_copy(src, dst, in_sem.at[i])
        for i, (src, dst) in enumerate(
            [
                (rank_hbm, rank_ref), (rows_hbm, rows_ref), (count_hbm, count_ref),
                (k_hbm, k_ref), (v_hbm, v_ref), (sink_hbm, sink_ref),
                (q_hbm, q_ref), (g_hbm, g_ref),
            ]
        )
    ]
    for load in loads:
        load.start()
    for load in loads[:5]:
        load.wait()

    picked = rows_ref[0, 0]
    hit = lax.broadcasted_iota(jnp.int32, (8, length), 1) == picked
    one_hot = jnp.where(hit, 1.0, 0.0).astype(bf16)
    own_bucket = jnp.where(rank_ref[...] >= BUCKET, 1.0, 0.0)
    mark = jnp.sum(jnp.where(hit, own_bucket, 0.0), axis=1, keepdims=True)
    row_buf[:, :WIDTH] = jnp.dot(one_hot, k_ref[...], preferred_element_type=f32)
    row_buf[:, WIDTH : 2 * WIDTH] = jnp.dot(one_hot, v_ref[...], preferred_element_type=f32)
    tail = lax.broadcasted_iota(jnp.int32, (8, 128), 1)
    row_buf[:, 2 * WIDTH :] = jnp.where(
        tail == 0, count_ref[0, 0].astype(f32), jnp.where(tail == 1, mark, 0.0)
    )
    rows1[pl.ds(x, 1), :] = row_buf[0:1, :]
    pl.semaphore_wait(barrier, len(peers))

    x_copies = [
        send(row_buf.at[pl.ds(0, 1)], rows1.at[pl.ds(x, 1)],
             x_send.at[d - 1], x_recv.at[d - 1], x_peer(d))
        for d in range(1, nx)
    ]
    pair_copies = [
        send(rank_ref, far_rank, pair_send.at[0], pair_recv.at[0], partner),
        send(k_ref, far_k, pair_send.at[1], pair_recv.at[1], partner),
        send(v_ref, far_v, pair_send.at[2], pair_recv.at[2], partner),
    ]
    for load in loads[5:]:
        load.wait()

    up = lax.broadcasted_iota(jnp.int32, (length, length), 0)
    across = lax.broadcasted_iota(jnp.int32, (length, length), 1)

    def inside(line):
        upright = jnp.sum(jnp.where(up == across, line, 0.0), axis=1, keepdims=True)
        return jnp.concatenate([jnp.where(upright == own_bucket, 0.0, NEG)] * GROUP, 1)

    def heads_of(ref, j):
        first = j * GROUP * HDIM
        return jnp.concatenate(
            [ref[:, first + h * HDIM : first + (h + 1) * HDIM] for h in range(GROUP)], 0
        )

    def across_dot(left, right):
        return lax.dot_general(
            left, right, (((1,), (1,)), ((), ())), preferred_element_type=f32
        )

    def sink_of(j):
        return jnp.concatenate(
            [jnp.full((1, length), sink_ref[j * GROUP + h], f32) for h in range(GROUP)], 1
        )

    def score_block(which, keys, values, bias, j):
        cut = slice(j * HDIM, (j + 1) * HDIM)
        score = across_dot(keys[:, cut], heads_of(q_ref, j)) * scale + bias
        lift = across_dot(values[:, cut], heads_of(g_ref, j))
        top = jnp.max(score, axis=0, keepdims=True)
        weight = jnp.exp(score - top)
        weights[j, which] = weight
        lifts[j, which] = lift
        stats[j, 3 * which : 3 * which + 1] = top
        stats[j, 3 * which + 1 : 3 * which + 2] = jnp.sum(weight, axis=0, keepdims=True)
        stats[j, 3 * which + 2 : 3 * which + 3] = jnp.sum(weight * lift, axis=0, keepdims=True)

    own_bias = inside(own_bucket)
    for j in range(EARLY):
        score_block(0, k_ref, v_ref, own_bias, j)
    arrived(x_copies)
    blk_buf[...] = rows1[...].astype(bf16)
    samples[y] = rows1[...].astype(bf16)
    y_copies = [
        send(blk_buf, samples.at[y], y_send.at[d - 1], y_recv.at[d - 1], y_peer(d))
        for d in range(1, ny)
    ]
    for j in range(EARLY, KV_HEADS):
        score_block(0, k_ref, v_ref, own_bias, j)
    arrived(pair_copies)
    far_bias = inside(jnp.where(far_rank[...] >= BUCKET, 1.0, 0.0))
    for j in range(KV_HEADS):
        score_block(1, far_k, far_v, far_bias, j)
    arrived(y_copies)

    panel = jnp.concatenate([samples[i].astype(f32) for i in range(ny)], 0)
    panel_kv = panel[:, : 2 * WIDTH].astype(bf16)
    counts = panel[:, 2 * WIDTH : 2 * WIDTH + 1]
    marks = panel[:, 2 * WIDTH + 1 : 2 * WIDTH + 2]
    slot = lax.broadcasted_iota(jnp.int32, (slots, 1), 0)
    near = jnp.where(slot // 2 == ctx // 2, marks, 2.0)
    bias = jnp.concatenate([jnp.where(near == own_bucket, NEG, jnp.log(counts))] * GROUP, 1)
    sink_lane = lax.broadcasted_iota(jnp.int32, (1, 128), 1)
    sink_line = jnp.zeros((1, 128), f32)
    t_copies = []
    for j in range(KV_HEADS):
        low = j * HDIM
        q_part, g_part = heads_of(q_ref, j), heads_of(g_ref, j)
        score = across_dot(panel_kv[:, low : low + HDIM], q_part) * scale + bias
        lift = across_dot(panel_kv[:, WIDTH + low : WIDTH + low + HDIM], g_part)
        sink_row = sink_of(j)
        own_top, far_top = stats[j, 0:1], stats[j, 3:4]
        top = jnp.maximum(
            jnp.maximum(own_top, far_top),
            jnp.maximum(jnp.max(score, axis=0, keepdims=True), sink_row),
        )
        weight = jnp.exp(score - top)
        own_part, far_part = jnp.exp(own_top - top), jnp.exp(far_top - top)
        sink_weight = jnp.exp(sink_row - top)
        inverse = 1.0 / (
            own_part * stats[j, 1:2] + far_part * stats[j, 4:5]
            + jnp.sum(weight, axis=0, keepdims=True) + sink_weight
        )
        delta = inverse * (
            own_part * stats[j, 2:3] + far_part * stats[j, 5:6]
            + jnp.sum(weight * lift, axis=0, keepdims=True)
        )
        chance = weight * inverse
        ds_t = (chance * (lift - delta)).astype(bf16)
        dscore[j, 2 * length :] = ds_t
        stats[j, 0:1] = own_part * inverse
        stats[j, 3:4] = far_part * inverse
        stats[j, 6:7] = delta
        key_all = jnp.dot(ds_t, q_part, preferred_element_type=f32) * scale
        value_all = jnp.dot(chance.astype(bf16), g_part, preferred_element_type=f32)
        for i in range(ny):
            terms[j, i, :, :HDIM] = key_all[i * nx : (i + 1) * nx].astype(bf16)
            terms[j, i, :, HDIM:] = value_all[i * nx : (i + 1) * nx].astype(bf16)
        terms_in[j, y] = terms[j, y]
        for d in range(1, ny):
            t_copies.append(send(
                terms.at[j, (y + d) % ny], terms_in.at[j, y],
                t_send.at[j, d - 1], t_recv.at[j, d - 1], y_peer(d),
            ))
        sink_term = sink_weight * inverse * delta
        for h in range(GROUP):
            part = jnp.sum(sink_term[:, h * length : (h + 1) * length], axis=1, keepdims=True)
            sink_line = jnp.where(sink_lane == j * GROUP + h, part, sink_line)
    sink_buf[...] = sink_line
    sink_dp[pl.ds(dp, 1), :] = sink_line
    dp_copies = [
        send(sink_buf, sink_dp.at[pl.ds(dp, 1)], sd_send.at[d - 1], sd_recv.at[d - 1], dp_peer(d))
        for d in range(1, ndp)
    ]

    def gradients(which, j):
        chance = weights[j, which] * stats[j, 3 * which : 3 * which + 1]
        ds_t = (chance * (lifts[j, which] - stats[j, 6:7])).astype(bf16)
        dscore[j, which * length : (which + 1) * length] = ds_t
        key_part = jnp.dot(ds_t, heads_of(q_ref, j), preferred_element_type=f32) * scale
        value_part = jnp.dot(chance.astype(bf16), heads_of(g_ref, j), preferred_element_type=f32)
        return key_part, value_part

    back_copies = []
    for j in range(KV_HEADS):
        key_part, value_part = gradients(1, j)
        back_buf[j, :, :HDIM] = key_part.astype(bf16)
        back_buf[j, :, HDIM:] = value_part.astype(bf16)
        back_copies.append(send(
            back_buf.at[j], back.at[j], back_send.at[j], back_recv.at[j], partner
        ))

    def own_gradients(j):
        cut = slice(j * HDIM, (j + 1) * HDIM)
        own_k[:, cut], own_v[:, cut] = gradients(0, j)

    def query_gradients(j):
        low = j * HDIM
        keys = jnp.concatenate(
            [k_ref[:, low : low + HDIM], far_k[:, low : low + HDIM], panel_kv[:, low : low + HDIM]], 0
        )
        query_part = scale * lax.dot_general(
            dscore[j], keys, (((0,), (0,)), ((), ())), preferred_element_type=f32
        )
        for h in range(GROUP):
            first = (j * GROUP + h) * HDIM
            dq_ref[:, first : first + HDIM] = query_part[h * length : (h + 1) * length].astype(bf16)

    for j in range(KV_HEADS):
        own_gradients(j)
    arrived(dp_copies)
    sink_sum = jnp.sum(sink_dp[...], axis=0, keepdims=True)
    sink_part[...] = sink_sum
    sink_y[pl.ds(y, 1), :] = sink_sum
    sy_copies = [
        send(sink_part, sink_y.at[pl.ds(y, 1)], sy_send.at[d - 1], sy_recv.at[d - 1], y_peer(d))
        for d in range(1, ny)
    ]
    for j in range(KV_HEADS // 2):
        query_gradients(j)
    arrived(t_copies)
    for j in range(KV_HEADS):
        total = terms_in[j, 0].astype(f32)
        for i in range(1, ny):
            total = total + terms_in[j, i].astype(f32)
        lines[:, j * HDIM : (j + 1) * HDIM] = total[:, :HDIM]
        lines[:, WIDTH + j * HDIM : WIDTH + (j + 1) * HDIM] = total[:, HDIM:]
    lines_in[pl.ds(x, 1), :] = lines[pl.ds(x, 1), :]
    l_copies = [
        send(lines.at[pl.ds((x + d) % nx, 1)], lines_in.at[pl.ds(x, 1)],
             l_send.at[d - 1], l_recv.at[d - 1], x_peer(d))
        for d in range(1, nx)
    ]
    arrived(sy_copies)
    sink_sum = jnp.sum(sink_y[...], axis=0, keepdims=True)
    sink_last[...] = sink_sum
    sink_x[pl.ds(x, 1), :] = sink_sum
    sx_copies = [
        send(sink_last, sink_x.at[pl.ds(x, 1)], sx_send.at[d - 1], sx_recv.at[d - 1], x_peer(d))
        for d in range(1, nx)
    ]
    for j in range(KV_HEADS // 2, KV_HEADS):
        query_gradients(j)
    arrived(back_copies)
    arrived(l_copies)
    line = jnp.sum(lines_in[...], axis=0, keepdims=True)
    here = lax.broadcasted_iota(jnp.int32, (length, HDIM), 0) == picked
    for j in range(KV_HEADS):
        cut = slice(j * HDIM, (j + 1) * HDIM)
        dk_ref[:, cut] = (
            own_k[:, cut] + back[j, :, :HDIM].astype(f32) + jnp.where(here, line[:, cut], 0.0)
        ).astype(bf16)
        dv_ref[:, cut] = (
            own_v[:, cut]
            + back[j, :, HDIM:].astype(f32)
            + jnp.where(here, line[:, WIDTH + j * HDIM : WIDTH + (j + 1) * HDIM], 0.0)
        ).astype(bf16)
    arrived(sx_copies)
    ds_ref[...] = -jnp.sum(sink_x[...], axis=0, keepdims=True)
    for copy in started:
        copy.wait_send()


def store_kernel(dq_ref, dk_ref, dv_ref, ds_ref, dq_out, dk_out, dv_out, ds_out, out_sem):
    copies = [
        pltpu.make_async_copy(src, dst, out_sem.at[i])
        for i, (src, dst) in enumerate([(dq_ref, dq_out), (dk_ref, dk_out), (dv_ref, dv_out)])
    ]
    for copy in copies:
        copy.start()
    ds_out[...] = ds_ref[:, :HEADS]
    for copy in copies:
        copy.wait()


def on_device(
    ndp, query_rows, key_rows, value_rows, grad_rows, bucket_rank, sample_rows, sample_count, sink_logit
):
    length = query_rows.shape[1]
    slots = lax.axis_size("ctx")
    nx = 8 if slots >= 64 else 2
    ny = slots // nx
    keys = 2 * length + slots
    wide = GROUP * length
    f32, bf16, i32 = jnp.float32, jnp.bfloat16, jnp.int32
    vmem, smem, dma = pltpu.VMEM, pltpu.SMEM, pltpu.SemaphoreType.DMA
    space = pl.BlockSpec(memory_space=pltpu.VMEM)
    far = pl.BlockSpec(memory_space=pltpu.HBM)
    grads = [
        jax.ShapeDtypeStruct((length, HEADS * HDIM), bf16),
        jax.ShapeDtypeStruct((length, WIDTH), bf16),
        jax.ShapeDtypeStruct((length, WIDTH), bf16),
    ]
    results = pl.pallas_call(
        functools.partial(whole_kernel, ny, nx, ndp),
        out_shape=grads + [jax.ShapeDtypeStruct((1, 128), f32)],
        in_specs=[far] * 8,
        out_specs=[space] * 4,
        scratch_shapes=[
            vmem((length, HEADS * HDIM), bf16),
            vmem((length, WIDTH), bf16),
            vmem((length, WIDTH), bf16),
            vmem((length, HEADS * HDIM), bf16),
            vmem((1, length), i32),
            smem((1, 1), i32),
            smem((1, 1), i32),
            smem((HEADS,), f32),
            vmem((8, ROW), f32),
            vmem((nx, ROW), f32),
            vmem((nx, ROW), bf16),
            vmem((ny, nx, ROW), bf16),
            vmem((length, WIDTH), bf16),
            vmem((length, WIDTH), bf16),
            vmem((1, length), i32),
            vmem((KV_HEADS, 2, length, wide), f32),
            vmem((KV_HEADS, 2, length, wide), f32),
            vmem((KV_HEADS, 8, wide), f32),
            vmem((KV_HEADS, keys, wide), bf16),
            vmem((length, WIDTH), f32),
            vmem((length, WIDTH), f32),
            vmem((KV_HEADS, length, 2 * HDIM), bf16),
            vmem((KV_HEADS, length, 2 * HDIM), bf16),
            vmem((KV_HEADS, ny, nx, 2 * HDIM), bf16),
            vmem((KV_HEADS, ny, nx, 2 * HDIM), bf16),
            vmem((nx, 2 * WIDTH), f32),
            vmem((nx, 2 * WIDTH), f32),
            vmem((1, 128), f32),
            vmem((ndp, 128), f32),
            vmem((1, 128), f32),
            vmem((ny, 128), f32),
            vmem((1, 128), f32),
            vmem((nx, 128), f32),
            dma((8,)),
            dma((nx - 1,)), dma((nx - 1,)),
            dma((ny - 1,)), dma((ny - 1,)),
            dma((3,)), dma((3,)),
            dma((KV_HEADS,)), dma((KV_HEADS,)),
            dma((KV_HEADS, ny - 1)), dma((KV_HEADS, ny - 1)),
            dma((nx - 1,)), dma((nx - 1,)),
            dma((ndp - 1,)), dma((ndp - 1,)),
            dma((ny - 1,)), dma((ny - 1,)),
            dma((nx - 1,)), dma((nx - 1,)),
        ],
        compiler_params=pltpu.CompilerParams(
            collective_id=0, has_side_effects=True, vmem_limit_bytes=40 << 20
        ),
    )(
        query_rows[0], key_rows[0], value_rows[0], grad_rows[0],
        bucket_rank, sample_rows, sample_count, sink_logit,
    )
    dq, dk, dv, ds = pl.pallas_call(
        store_kernel,
        out_shape=grads + [jax.ShapeDtypeStruct((1, HEADS), f32)],
        in_specs=[space] * 4,
        out_specs=[far] * 3 + [space],
        scratch_shapes=[dma((3,))],
        compiler_params=pltpu.CompilerParams(vmem_limit_bytes=8 << 20),
    )(*results)
    return dq[None], dk[None], dv[None], ds[0]


def solution(mesh):
    return jax.shard_map(
        functools.partial(on_device, mesh.shape["dp"]),
        mesh=mesh,
        in_specs=(
            P("dp", "ctx", None),
            P("dp", "ctx", None),
            P("dp", "ctx", None),
            P("dp", "ctx", None),
            P("dp", "ctx"),
            P("dp", "ctx"),
            P("dp", "ctx"),
            P(),
        ),
        out_specs=(P("dp", "ctx", None), P("dp", "ctx", None), P("dp", "ctx", None), P()),
        check_vma=False,
    )
```

time: 57.9 us -> 56.5 us (0.976)
  the two profiles are of different devices: /device:TPU:8 before, /device:TPU:2 now
where the time goes in v2:
time: 56.5 us; the launch traced here: 56.2 us
  Pallas kernels  49.7 us (88%)
  local copies, waits for them, and re-layouts  4.55 us (8%)
  between operations  1.95 us (3%)
    pallas_call x1, Pallas kernels, on_device(): pl.pallas_call(functools.partial(whole_kernel, ny, nx, ndp), out_shape=gr...  48.3 us
    unnamed x12, local copies, waits for them, and re-layouts  4.55 us
    pallas_call x1, Pallas kernels, on_device(): pl.pallas_call(store_kernel, out_shape=grads + [jax.ShapeDtypeStruct((1,...  1.41 us

profile of v2, /device:TPU:2, one launch (start us, length us, event | category | flops | bytes accessed | tf_op | source)
XLA Modules:
  0.0 56.2 jit_solution(3966658686420613472)
XLA Ops:
  1.9 0.0 copy-start.4
  1.9 0.0 copy-start.5
  1.9 0.6 %copy-done.4 = s32[1,128]{1,0:T(1,128)S(1)} copy-done((s32[1,128]{1,0:T(1,128)S(1)}, s32[1,128]{1,0:T(1,128)}, u32[]{:S(2)}) %copy-start.4) | copy-done | bytes 536
  2.6 0.0 copy-done.5
  2.6 0.0 copy-start
  2.6 1.0 %copy-done = bf16[1,128,2048]{2,1,0:T(8,128)(2,1)S(1)} copy-done((bf16[1,128,2048]{2,1,0:T(8,128)(2,1)S(1)}, bf16[1,128,2048]{2,1,0:T(8,128)(2,1)}, u32[]{:S(2)}) %copy-start) | copy-done | bytes 524312
  3.6 0.0 copy-start.1
  3.6 1.0 %copy-done.1 = bf16[1,128,2048]{2,1,0:T(8,128)(2,1)S(1)} copy-done((bf16[1,128,2048]{2,1,0:T(8,128)(2,1)S(1)}, bf16[1,128,2048]{2,1,0:T(8,128)(2,1)}, u32[]{:S(2)}) %copy-start.1) | copy-done | bytes 524312
  4.7 0.0 copy-start.2
  4.7 0.9 %copy-done.2 = bf16[1,128,512]{2,1,0:T(8,128)(2,1)S(1)} copy-done((bf16[1,128,512]{2,1,0:T(8,128)(2,1)S(1)}, bf16[1,128,512]{2,1,0:T(8,128)(2,1)}, u32[]{:S(2)}) %copy-start.2) | copy-done | bytes 131096
  5.6 0.0 copy-start.3
  5.6 0.9 %copy-done.3 = bf16[1,128,512]{2,1,0:T(8,128)(2,1)S(1)} copy-done((bf16[1,128,512]{2,1,0:T(8,128)(2,1)S(1)}, bf16[1,128,512]{2,1,0:T(8,128)(2,1)}, u32[]{:S(2)}) %copy-start.3) | copy-done | bytes 131096
  6.5 48.3 %shard_map.111 = (bf16[128,2048]{1,0:T(8,128)(2,1)S(1)}, bf16[128,512]{1,0:T(8,128)(2,1)S(1)}, bf16[128,512]{1,0:T(8,128)(2,1)S(1)}, f32[1,128]{1,0:T(1,128)S(1)}) custom-call(bf16[128,2048]{1,0:T(8,128)(2,1)S(1)} %bitcast.8, bf16[128,512]{1,0:T(8,128)(2,1)S(1)} %bitcast.10, bf16[128,512]{1,0:T(8,128)(2,1)S(1)} %bitcast.11, bf16[128,2048]{1,0:T(8,128)(2,1)S(1)} %bitcast.9, ...), custom_call_target="tpu_custom_call" | custom-call | tf_op jit(solution)/shard_map/pallas_call | solution.py:348
  54.8 1.4 %shard_map.112 = (bf16[128,2048]{1,0:T(8,128)(2,1)}, bf16[128,512]{1,0:T(8,128)(2,1)}, bf16[128,512]{1,0:T(8,128)(2,1)}, f32[1,16]{1,0:T(1,128)}) custom-call(bf16[128,2048]{1,0:T(8,128)(2,1)S(1)} %get-tuple-element.12.dq_ref, bf16[128,512]{1,0:T(8,128)(2,1)S(1)} %get-tuple-element.13.dk_ref, bf16[128,512]{1,0:T(8,128)(2,1)S(1)} %get-tuple-element.14.dv_ref, ...), custom_call_target="tpu_custom_call" | custom-call | tf_op jit(solution)/shard_map/pallas_call | solution.py:405
Async XLA Ops:
  1.9 0.7 %copy-start.4 = (s32[1,128]{1,0:T(1,128)S(1)}, s32[1,128]{1,0:T(1,128)}, u32[]{:S(2)}) copy-start(s32[1,128]{1,0:T(1,128)} %rank_hbm.1) | copy-start | bytes 1540
  1.9 0.7 %copy-start.5 = (f32[16]{0:T(128)S(1)}, f32[16]{0:T(128)}, u32[]{:S(2)}) copy-start(f32[16]{0:T(128)} %sink_hbm.1) | copy-start | bytes 196
  2.6 1.0 %copy-start = (bf16[1,128,2048]{2,1,0:T(8,128)(2,1)S(1)}, bf16[1,128,2048]{2,1,0:T(8,128)(2,1)}, u32[]{:S(2)}) copy-start(bf16[1,128,2048]{2,1,0:T(8,128)(2,1)} %param.8) | copy-start | bytes 1572868
  3.6 1.0 %copy-start.1 = (bf16[1,128,2048]{2,1,0:T(8,128)(2,1)S(1)}, bf16[1,128,2048]{2,1,0:T(8,128)(2,1)}, u32[]{:S(2)}) copy-start(bf16[1,128,2048]{2,1,0:T(8,128)(2,1)} %param.11) | copy-start | bytes 1572868
  4.7 0.9 %copy-start.2 = (bf16[1,128,512]{2,1,0:T(8,128)(2,1)S(1)}, bf16[1,128,512]{2,1,0:T(8,128)(2,1)}, u32[]{:S(2)}) copy-start(bf16[1,128,512]{2,1,0:T(8,128)(2,1)} %param.9) | copy-start | bytes 393220
  5.6 0.9 %copy-start.3 = (bf16[1,128,512]{2,1,0:T(8,128)(2,1)S(1)}, bf16[1,128,512]{2,1,0:T(8,128)(2,1)}, u32[]{:S(2)}) copy-start(bf16[1,128,512]{2,1,0:T(8,128)(2,1)} %param.10) | copy-start | bytes 393220

commit v3 on v2

--- a/solution.py
+++ b/solution.py
@@ -25,7 +25,7 @@
     dq_ref, dk_ref, dv_ref, ds_ref,
     q_ref, k_ref, v_ref, g_ref, rank_ref, rows_ref, count_ref, sink_ref,
     row_buf, rows1, blk_buf, samples, far_k, far_v, far_rank,
-    weights, lifts, stats, dscore, own_k, own_v, back_buf, back,
+    weights, lifts, stats, dscore, sample_prob, own_k, own_v, back_buf, back,
     terms, terms_in, lines, lines_in,
     sink_buf, sink_dp, sink_part, sink_y, sink_last, sink_x,
     in_sem, x_send, x_recv, y_send, y_recv, pair_send, pair_recv,
@@ -64,6 +64,18 @@
         for copy in copies:
             copy.wait_recv()
 
+    loads = [
+        pltpu.make_async_copy(src, dst, in_sem.at[i])
+        for i, (src, dst) in enumerate(
+            [
+                (rank_hbm, rank_ref), (rows_hbm, rows_ref), (count_hbm, count_ref),
+                (k_hbm, k_ref), (v_hbm, v_ref), (sink_hbm, sink_ref),
+                (q_hbm, q_ref), (g_hbm, g_ref),
+            ]
+        )
+    ]
+    for load in loads:
+        load.start()
     barrier = pltpu.get_barrier_semaphore()
     peers = (
         [x_peer(d) for d in range(1, nx)]
@@ -72,18 +84,6 @@
     )
     for peer in peers:
         pl.semaphore_signal(barrier, inc=1, device_id=peer, device_id_type=MESH)
-    loads = [
-        pltpu.make_async_copy(src, dst, in_sem.at[i])
-        for i, (src, dst) in enumerate(
-            [
-                (rank_hbm, rank_ref), (rows_hbm, rows_ref), (count_hbm, count_ref),
-                (k_hbm, k_ref), (v_hbm, v_ref), (sink_hbm, sink_ref),
-                (q_hbm, q_ref), (g_hbm, g_ref),
-            ]
-        )
-    ]
-    for load in loads:
-        load.start()
     for load in loads[:5]:
         load.wait()
 
@@ -176,7 +176,6 @@
     bias = jnp.concatenate([jnp.where(near == own_bucket, NEG, jnp.log(counts))] * GROUP, 1)
     sink_lane = lax.broadcasted_iota(jnp.int32, (1, 128), 1)
     sink_line = jnp.zeros((1, 128), f32)
-    t_copies = []
     for j in range(KV_HEADS):
         low = j * HDIM
         q_part, g_part = heads_of(q_ref, j), heads_of(g_ref, j)
@@ -205,8 +204,24 @@
         stats[j, 0:1] = own_part * inverse
         stats[j, 3:4] = far_part * inverse
         stats[j, 6:7] = delta
-        key_all = jnp.dot(ds_t, q_part, preferred_element_type=f32) * scale
-        value_all = jnp.dot(chance.astype(bf16), g_part, preferred_element_type=f32)
+        sample_prob[j] = chance.astype(bf16)
+        sink_term = sink_weight * inverse * delta
+        for h in range(GROUP):
+            part = jnp.sum(sink_term[:, h * length : (h + 1) * length], axis=1, keepdims=True)
+            sink_line = jnp.where(sink_lane == j * GROUP + h, part, sink_line)
+    sink_buf[...] = sink_line
+    sink_dp[pl.ds(dp, 1), :] = sink_line
+    dp_copies = [
+        send(sink_buf, sink_dp.at[pl.ds(dp, 1)], sd_send.at[d - 1], sd_recv.at[d - 1], dp_peer(d))
+        for d in range(1, ndp)
+    ]
+
+    t_copies = []
+    for j in range(KV_HEADS):
+        key_all = jnp.dot(
+            dscore[j, 2 * length :], heads_of(q_ref, j), preferred_element_type=f32) * scale
+        value_all = jnp.dot(
+            sample_prob[j], heads_of(g_ref, j), preferred_element_type=f32)
         for i in range(ny):
             terms[j, i, :, :HDIM] = key_all[i * nx : (i + 1) * nx].astype(bf16)
             terms[j, i, :, HDIM:] = value_all[i * nx : (i + 1) * nx].astype(bf16)
@@ -216,16 +231,6 @@
                 terms.at[j, (y + d) % ny], terms_in.at[j, y],
                 t_send.at[j, d - 1], t_recv.at[j, d - 1], y_peer(d),
             ))
-        sink_term = sink_weight * inverse * delta
-        for h in range(GROUP):
-            part = jnp.sum(sink_term[:, h * length : (h + 1) * length], axis=1, keepdims=True)
-            sink_line = jnp.where(sink_lane == j * GROUP + h, part, sink_line)
-    sink_buf[...] = sink_line
-    sink_dp[pl.ds(dp, 1), :] = sink_line
-    dp_copies = [
-        send(sink_buf, sink_dp.at[pl.ds(dp, 1)], sd_send.at[d - 1], sd_recv.at[d - 1], dp_peer(d))
-        for d in range(1, ndp)
-    ]
 
     def gradients(which, j):
         chance = weights[j, which] * stats[j, 3 * which : 3 * which + 1]
@@ -260,8 +265,6 @@
             first = (j * GROUP + h) * HDIM
             dq_ref[:, first : first + HDIM] = query_part[h * length : (h + 1) * length].astype(bf16)
 
-    for j in range(KV_HEADS):
-        own_gradients(j)
     arrived(dp_copies)
     sink_sum = jnp.sum(sink_dp[...], axis=0, keepdims=True)
     sink_part[...] = sink_sum
@@ -270,8 +273,8 @@
         send(sink_part, sink_y.at[pl.ds(y, 1)], sy_send.at[d - 1], sy_recv.at[d - 1], y_peer(d))
         for d in range(1, ny)
     ]
-    for j in range(KV_HEADS // 2):
-        query_gradients(j)
+    for j in range(KV_HEADS):
+        own_gradients(j)
     arrived(t_copies)
     for j in range(KV_HEADS):
         total = terms_in[j, 0].astype(f32)
@@ -293,7 +296,7 @@
         send(sink_last, sink_x.at[pl.ds(x, 1)], sx_send.at[d - 1], sx_recv.at[d - 1], x_peer(d))
         for d in range(1, nx)
     ]
-    for j in range(KV_HEADS // 2, KV_HEADS):
+    for j in range(KV_HEADS):
         query_gradients(j)
     arrived(back_copies)
     arrived(l_copies)
@@ -370,6 +373,7 @@
             vmem((KV_HEADS, 2, length, wide), f32),
             vmem((KV_HEADS, 8, wide), f32),
             vmem((KV_HEADS, keys, wide), bf16),
+            vmem((KV_HEADS, slots, wide), bf16),
             vmem((length, WIDTH), f32),
             vmem((length, WIDTH), f32),
             vmem((KV_HEADS, length, 2 * HDIM), bf16),
@@ -399,8 +403,14 @@
             collective_id=0, has_side_effects=True, vmem_limit_bytes=40 << 20
         ),
     )(
-        query_rows[0], key_rows[0], value_rows[0], grad_rows[0],
-        bucket_rank, sample_rows, sample_count, sink_logit,
+        *[
+            pltpu.with_memory_space_constraint(array, pltpu.HBM)
+            for array in (
+                query_rows[0], key_rows[0], value_rows[0], grad_rows[0], bucket_rank
+            )
+        ],
+        sample_rows, sample_count,
+        pltpu.with_memory_space_constraint(sink_logit, pltpu.HBM),
     )
     dq, dk, dv, ds = pl.pallas_call(
         store_kernel,

time: 56.5 us -> 50.6 us (0.90)
  local copies, waits for them, and re-layouts: 4.55 us -> 0 us
  Pallas kernels: 49.7 us -> 48.5 us
    unnamed x12 -> x0, local copies, waits for them, and re-layouts: 4.55 us -> none
    pallas_call x1, Pallas kernels: 48.3 us -> 47.1 us  [on_device(): pl.pallas_call(functools.partial(whole_kernel, ny, nx, ndp), out_shape=gr...]
where the time goes in v3:
time: 50.6 us; the launch traced here: 50.4 us
  Pallas kernels  48.5 us (96%)
  between operations  1.93 us (4%)
    pallas_call x1, Pallas kernels, on_device(): pl.pallas_call(functools.partial(whole_kernel, ny, nx, ndp), out_shape=gr...  47.1 us
    pallas_call x1, Pallas kernels, on_device(): pl.pallas_call(store_kernel, out_shape=grads + [jax.ShapeDtypeStruct((1,...  1.41 us

profile of v3, /device:TPU:2, one launch (start us, length us, event | category | flops | bytes accessed | tf_op | source)
XLA Modules:
  0.0 50.4 jit_solution(13555520783960011108)
XLA Ops:
  1.9 47.1 %shard_map.111 = (bf16[128,2048]{1,0:T(8,128)(2,1)S(1)}, bf16[128,512]{1,0:T(8,128)(2,1)S(1)}, bf16[128,512]{1,0:T(8,128)(2,1)S(1)}, f32[1,128]{1,0:T(1,128)S(1)}) custom-call(bf16[128,2048]{1,0:T(8,128)(2,1)} %bitcast.8, bf16[128,512]{1,0:T(8,128)(2,1)} %bitcast.10, bf16[128,512]{1,0:T(8,128)(2,1)} %bitcast.11, bf16[128,2048]{1,0:T(8,128)(2,1)} %bitcast.9, ...), custom_call_target="tpu_custom_call" | custom-call | tf_op jit(solution)/shard_map/pallas_call | solution.py:351
  49.0 1.4 %shard_map.112 = (bf16[128,2048]{1,0:T(8,128)(2,1)}, bf16[128,512]{1,0:T(8,128)(2,1)}, bf16[128,512]{1,0:T(8,128)(2,1)}, f32[1,16]{1,0:T(1,128)}) custom-call(bf16[128,2048]{1,0:T(8,128)(2,1)S(1)} %get-tuple-element.12.dq_ref, bf16[128,512]{1,0:T(8,128)(2,1)S(1)} %get-tuple-element.13.dk_ref, bf16[128,512]{1,0:T(8,128)(2,1)S(1)} %get-tuple-element.14.dv_ref, ...), custom_call_target="tpu_custom_call" | custom-call | tf_op jit(solution)/shard_map/pallas_call | solution.py:415

commit v4 on v3

--- a/solution.py
+++ b/solution.py
@@ -16,6 +16,7 @@
 ROW = 2 * WIDTH + 128
 NEG = -1e30
 EARLY = 1
+FAR_FIRST = 2
 MESH = pl.DeviceIdType.MESH
 
 
@@ -77,10 +78,13 @@
     for load in loads:
         load.start()
     barrier = pltpu.get_barrier_semaphore()
+    def outward(size):
+        return sorted(range(1, size), key=lambda d: -min(d, size - d))
+
     peers = (
-        [x_peer(d) for d in range(1, nx)]
-        + [y_peer(d) for d in range(1, ny)]
-        + [dp_peer(d) for d in range(1, ndp)]
+        [x_peer(d) for d in outward(nx)]
+        + [y_peer(d) for d in outward(ny)]
+        + [dp_peer(d) for d in outward(ndp)]
     )
     for peer in peers:
         pl.semaphore_signal(barrier, inc=1, device_id=peer, device_id_type=MESH)
@@ -104,7 +108,7 @@
     x_copies = [
         send(row_buf.at[pl.ds(0, 1)], rows1.at[pl.ds(x, 1)],
              x_send.at[d - 1], x_recv.at[d - 1], x_peer(d))
-        for d in range(1, nx)
+        for d in outward(nx)
     ]
     pair_copies = [
         send(rank_ref, far_rank, pair_send.at[0], pair_recv.at[0], partner),
@@ -157,7 +161,7 @@
     samples[y] = rows1[...].astype(bf16)
     y_copies = [
         send(blk_buf, samples.at[y], y_send.at[d - 1], y_recv.at[d - 1], y_peer(d))
-        for d in range(1, ny)
+        for d in outward(ny)
     ]
     for j in range(EARLY, KV_HEADS):
         score_block(0, k_ref, v_ref, own_bias, j)
@@ -213,24 +217,23 @@
     sink_dp[pl.ds(dp, 1), :] = sink_line
     dp_copies = [
         send(sink_buf, sink_dp.at[pl.ds(dp, 1)], sd_send.at[d - 1], sd_recv.at[d - 1], dp_peer(d))
-        for d in range(1, ndp)
-    ]
-
-    t_copies = []
+        for d in outward(ndp)
+    ]
+
     for j in range(KV_HEADS):
         key_all = jnp.dot(
             dscore[j, 2 * length :], heads_of(q_ref, j), preferred_element_type=f32) * scale
         value_all = jnp.dot(
             sample_prob[j], heads_of(g_ref, j), preferred_element_type=f32)
         for i in range(ny):
-            terms[j, i, :, :HDIM] = key_all[i * nx : (i + 1) * nx].astype(bf16)
-            terms[j, i, :, HDIM:] = value_all[i * nx : (i + 1) * nx].astype(bf16)
-        terms_in[j, y] = terms[j, y]
-        for d in range(1, ny):
-            t_copies.append(send(
-                terms.at[j, (y + d) % ny], terms_in.at[j, y],
-                t_send.at[j, d - 1], t_recv.at[j, d - 1], y_peer(d),
-            ))
+            terms[i, j, :, :HDIM] = key_all[i * nx : (i + 1) * nx].astype(bf16)
+            terms[i, j, :, HDIM:] = value_all[i * nx : (i + 1) * nx].astype(bf16)
+    terms_in[y] = terms[y]
+    t_copies = [
+        send(terms.at[(y + d) % ny], terms_in.at[y],
+             t_send.at[d - 1], t_recv.at[d - 1], y_peer(d))
+        for d in outward(ny)
+    ]
 
     def gradients(which, j):
         chance = weights[j, which] * stats[j, 3 * which : 3 * which + 1]
@@ -241,7 +244,7 @@
         return key_part, value_part
 
     back_copies = []
-    for j in range(KV_HEADS):
+    def far_gradients(j):
         key_part, value_part = gradients(1, j)
         back_buf[j, :, :HDIM] = key_part.astype(bf16)
         back_buf[j, :, HDIM:] = value_part.astype(bf16)
@@ -265,28 +268,32 @@
             first = (j * GROUP + h) * HDIM
             dq_ref[:, first : first + HDIM] = query_part[h * length : (h + 1) * length].astype(bf16)
 
+    for j in range(FAR_FIRST):
+        far_gradients(j)
     arrived(dp_copies)
     sink_sum = jnp.sum(sink_dp[...], axis=0, keepdims=True)
     sink_part[...] = sink_sum
     sink_y[pl.ds(y, 1), :] = sink_sum
     sy_copies = [
         send(sink_part, sink_y.at[pl.ds(y, 1)], sy_send.at[d - 1], sy_recv.at[d - 1], y_peer(d))
-        for d in range(1, ny)
-    ]
+        for d in outward(ny)
+    ]
+    for j in range(FAR_FIRST, KV_HEADS):
+        far_gradients(j)
     for j in range(KV_HEADS):
         own_gradients(j)
     arrived(t_copies)
     for j in range(KV_HEADS):
-        total = terms_in[j, 0].astype(f32)
+        total = terms_in[0, j].astype(f32)
         for i in range(1, ny):
-            total = total + terms_in[j, i].astype(f32)
+            total = total + terms_in[i, j].astype(f32)
         lines[:, j * HDIM : (j + 1) * HDIM] = total[:, :HDIM]
         lines[:, WIDTH + j * HDIM : WIDTH + (j + 1) * HDIM] = total[:, HDIM:]
     lines_in[pl.ds(x, 1), :] = lines[pl.ds(x, 1), :]
     l_copies = [
         send(lines.at[pl.ds((x + d) % nx, 1)], lines_in.at[pl.ds(x, 1)],
              l_send.at[d - 1], l_recv.at[d - 1], x_peer(d))
-        for d in range(1, nx)
+        for d in outward(nx)
     ]
     arrived(sy_copies)
     sink_sum = jnp.sum(sink_y[...], axis=0, keepdims=True)
@@ -294,7 +301,7 @@
     sink_x[pl.ds(x, 1), :] = sink_sum
     sx_copies = [
         send(sink_last, sink_x.at[pl.ds(x, 1)], sx_send.at[d - 1], sx_recv.at[d - 1], x_peer(d))
-        for d in range(1, nx)
+        for d in outward(nx)
     ]
     for j in range(KV_HEADS):
         query_gradients(j)
@@ -378,8 +385,8 @@
             vmem((length, WIDTH), f32),
             vmem((KV_HEADS, length, 2 * HDIM), bf16),
             vmem((KV_HEADS, length, 2 * HDIM), bf16),
-            vmem((KV_HEADS, ny, nx, 2 * HDIM), bf16),
-            vmem((KV_HEADS, ny, nx, 2 * HDIM), bf16),
+            vmem((ny, KV_HEADS, nx, 2 * HDIM), bf16),
+            vmem((ny, KV_HEADS, nx, 2 * HDIM), bf16),
             vmem((nx, 2 * WIDTH), f32),
             vmem((nx, 2 * WIDTH), f32),
             vmem((1, 128), f32),
@@ -393,7 +400,7 @@
             dma((ny - 1,)), dma((ny - 1,)),
             dma((3,)), dma((3,)),
             dma((KV_HEADS,)), dma((KV_HEADS,)),
-            dma((KV_HEADS, ny - 1)), dma((KV_HEADS, ny - 1)),
+            dma((ny - 1,)), dma((ny - 1,)),
             dma((nx - 1,)), dma((nx - 1,)),
             dma((ndp - 1,)), dma((ndp - 1,)),
             dma((ny - 1,)), dma((ny - 1,)),

time: 50.6 us -> 50.1 us (level)
  Pallas kernels: 48.5 us -> 47.9 us
    pallas_call x1, Pallas kernels: 47.1 us -> 46.5 us  [on_device(): pl.pallas_call(functools.partial(whole_kernel, ny, nx, ndp), out_shape=gr...]
where the time goes in v4:
time: 50.1 us; the launch traced here: 49.9 us
  Pallas kernels  47.9 us (96%)
  between operations  1.93 us (4%)
    pallas_call x1, Pallas kernels, on_device(): pl.pallas_call(functools.partial(whole_kernel, ny, nx, ndp), out_shape=gr...  46.5 us
    pallas_call x1, Pallas kernels, on_device(): pl.pallas_call(store_kernel, out_shape=grads + [jax.ShapeDtypeStruct((1,...  1.41 us

profile of v4, /device:TPU:2, one launch (start us, length us, event | category | flops | bytes accessed | tf_op | source)
XLA Modules:
  0.0 49.9 jit_solution(5002594564265447671)
XLA Ops:
  1.9 46.5 %shard_map.111 = (bf16[128,2048]{1,0:T(8,128)(2,1)S(1)}, bf16[128,512]{1,0:T(8,128)(2,1)S(1)}, bf16[128,512]{1,0:T(8,128)(2,1)S(1)}, f32[1,128]{1,0:T(1,128)S(1)}) custom-call(bf16[128,2048]{1,0:T(8,128)(2,1)} %bitcast.8, bf16[128,512]{1,0:T(8,128)(2,1)} %bitcast.10, bf16[128,512]{1,0:T(8,128)(2,1)} %bitcast.11, bf16[128,2048]{1,0:T(8,128)(2,1)} %bitcast.9, ...), custom_call_target="tpu_custom_call" | custom-call | tf_op jit(solution)/shard_map/pallas_call | solution.py:358
  48.5 1.4 %shard_map.112 = (bf16[128,2048]{1,0:T(8,128)(2,1)}, bf16[128,512]{1,0:T(8,128)(2,1)}, bf16[128,512]{1,0:T(8,128)(2,1)}, f32[1,16]{1,0:T(1,128)}) custom-call(bf16[128,2048]{1,0:T(8,128)(2,1)S(1)} %get-tuple-element.12.dq_ref, bf16[128,512]{1,0:T(8,128)(2,1)S(1)} %get-tuple-element.13.dk_ref, bf16[128,512]{1,0:T(8,128)(2,1)S(1)} %get-tuple-element.14.dv_ref, ...), custom_call_target="tpu_custom_call" | custom-call | tf_op jit(solution)/shard_map/pallas_call | solution.py:422
